TPU v7x, 32 devices: a whole 2x2x4 slice. The times are simulated.
32 devices in a mesh: dp: 8 (over z, x), tensor: 4 (over y, core).
Axes of the slice: x: 2, y: 2, z: 4, core: 2. Of those that a mesh axis runs over, the one named last changes fastest.
Arguments:
- tokens: bfloat16 [8192, 1024], P(('dp', 'tensor')), may hold values from -6 to 6
- attn_gain: float32 [1024], replicated, may hold values from 0.5 to 1.5
- qkv_weight: bfloat16 [1024, 16, 192], P('dp', 'tensor'), may hold values from -0.1875 to 0.1875
- out_weight: bfloat16 [1024, 1024], P('tensor', 'dp'), may hold values from -4 to 4
- mlp_gain: float32 [1024], replicated, may hold values from 0.5 to 1.5
- in_weight: bfloat16 [1024, 2, 2624], P('dp', None, 'tensor'), may hold values from -0.1875 to 0.1875
- down_weight: bfloat16 [2624, 1024], P('tensor', 'dp'), may hold values from -0.125 to 0.125
- seg_lengths: int32 [8, 3], P('dp'), may hold values from 1 to 512, 1024 in all within a row
- cotangent: bfloat16 [8192, 1024], P(('dp', 'tensor')), may hold values from -12 to 12
Outputs:
- layer_out: bfloat16 [8192, 1024], P(('dp', 'tensor'))
- grad_tokens: bfloat16 [8192, 1024], P(('dp', 'tensor'))
- grad_attn_gain: float32 [1024], replicated
- grad_qkv_weight: float32 [1024, 16, 192], P('dp', 'tensor')
- grad_out_weight: float32 [1024, 1024], P('tensor', 'dp')
- grad_mlp_gain: float32 [1024], replicated
- grad_in_weight: float32 [1024, 2, 2624], P('dp', None, 'tensor')
- grad_down_weight: float32 [2624, 1024], P('tensor', 'dp')
Inputs may be any that keep to these rules, and one draw needn't show every extreme that they name: `seg_lengths`: row p holds the lengths of the 3 segments that fill pack p in order; they sum to 1024 and the longest is 512.
All inputs are finite; a program needn't handle non-finite values.
Results may differ from a plain program's by a relative error of at most 0.024.
Values may be sent and summed in bfloat16 or wider, within the bound.
A program may use at most 128 MiB of HBM per device.

v0:
```python
import math
import jax
import jax.numpy as jnp
from jax import lax
from jax.sharding import PartitionSpec as P

NORM_EPS = 1e-05
ROPE_BASE = 160000.0
HALF_ROOT = 0.7071067811865476
INV_ROOT_TAU = 0.3989422804014327
MASKED_SCORE = -1e30


def dot_plain(left, right):
    return jnp.dot(left, right, preferred_element_type=jnp.float32)


def dot_first(left, right):
    return lax.dot_general(
        left, right, (((0,), (0,)), ((), ())), preferred_element_type=jnp.float32
    )


def dot_last(left, right):
    return lax.dot_general(
        left, right, (((1,), (1,)), ((), ())), preferred_element_type=jnp.float32
    )


def layer_norm(row_data, norm_gain):
    centered = row_data - jnp.mean(row_data, axis=-1, keepdims=True)
    inverse = lax.rsqrt(jnp.mean(centered * centered, axis=-1, keepdims=True) + NORM_EPS)
    unit_rows = centered * inverse
    return (unit_rows * norm_gain, unit_rows, inverse)


def norm_back(grad_normed, unit_rows, inverse, norm_gain):
    scaled = grad_normed * norm_gain
    grad_rows = inverse * (
        scaled
        - jnp.mean(scaled, axis=-1, keepdims=True)
        - unit_rows * jnp.mean(scaled * unit_rows, axis=-1, keepdims=True)
    )
    return (grad_rows, jnp.sum(grad_normed * unit_rows, axis=0))


def gelu_parts(value_in):
    normal_cdf = 0.5 * (1.0 + lax.erf(value_in * HALF_ROOT))
    slope = normal_cdf + value_in * INV_ROOT_TAU * jnp.exp(-0.5 * value_in * value_in)
    return (value_in * normal_cdf, slope)


def segment_info(seg_lens, pack_rows):
    seg_ends = jnp.cumsum(seg_lens)
    places = lax.iota(jnp.int32, pack_rows)
    before = seg_ends[None, :] <= places[:, None]
    seg_ids = jnp.sum(before.astype(jnp.int32), axis=1)
    seg_first = jnp.sum(jnp.where(before, seg_lens[None, :], 0), axis=1)
    return (seg_ids, places - seg_first)


def rotary(position, head_dim):
    half_dim = head_dim // 2
    inv_freq = jnp.exp(lax.iota(jnp.float32, half_dim) * (-2.0 * math.log(ROPE_BASE) / head_dim))
    angles = position.astype(jnp.float32)[:, None] * inv_freq[None, :]
    return (jnp.cos(angles), jnp.sin(angles))


def turn(vectors, cos_table, sin_table):
    half_dim = vectors.shape[-1] // 2
    front_half = vectors[..., :half_dim]
    back_half = vectors[..., half_dim:]
    cos_part = cos_table[:, None, :]
    sin_part = sin_table[:, None, :]
    return jnp.concatenate(
        [
            front_half * cos_part - back_half * sin_part,
            back_half * cos_part + front_half * sin_part,
        ],
        axis=-1,
    )


def turn_back(grads_in, cos_table, sin_table):
    half_dim = grads_in.shape[-1] // 2
    front_half = grads_in[..., :half_dim]
    back_half = grads_in[..., half_dim:]
    cos_part = cos_table[:, None, :]
    sin_part = sin_table[:, None, :]
    return jnp.concatenate(
        [
            front_half * cos_part + back_half * sin_part,
            back_half * cos_part - front_half * sin_part,
        ],
        axis=-1,
    )


def block_scores(query_part, key_part, seg_query, seg_key, score_scale):
    scores = (
        jnp.einsum("qhd,khd->hqk", query_part, key_part, preferred_element_type=jnp.float32)
        * score_scale
    )
    return jnp.where((seg_query[:, None] == seg_key[None, :])[None], scores, MASKED_SCORE)


def attention_forward(query_rows, key_rows, value_rows, seg_ids, query_block, score_scale):
    pack_rows, heads_local, head_dim = query_rows.shape
    block_count = pack_rows // query_block

    def one_block(block_index):
        query_start = block_index * query_block
        query_part = lax.dynamic_slice_in_dim(query_rows, query_start, query_block, 0)
        seg_query = lax.dynamic_slice_in_dim(seg_ids, query_start, query_block, 0)
        scores = block_scores(query_part, key_rows, seg_query, seg_ids, score_scale)
        row_top = jnp.max(scores, axis=-1, keepdims=True)
        expo = jnp.exp(scores - row_top)
        row_total = jnp.sum(expo, axis=-1, keepdims=True)
        weights = (expo / row_total).astype(jnp.bfloat16)
        result = jnp.einsum("hqk,khd->qhd", weights, value_rows, preferred_element_type=jnp.float32)
        return (result, (row_top + jnp.log(row_total))[..., 0])

    results, log_totals = lax.map(one_block, jnp.arange(block_count, dtype=jnp.int32))
    return (results.reshape(pack_rows, heads_local, head_dim), log_totals)


def attention_backward(
    query_rows, key_rows, value_rows, grad_attended, log_totals, seg_ids, query_block, score_scale
):
    pack_rows, heads_local, head_dim = query_rows.shape
    block_count = pack_rows // query_block

    def block_step(running, block_index):
        grad_keys, grad_values = running
        query_start = block_index * query_block
        query_part = lax.dynamic_slice_in_dim(query_rows, query_start, query_block, 0)
        grad_part = lax.dynamic_slice_in_dim(grad_attended, query_start, query_block, 0)
        seg_query = lax.dynamic_slice_in_dim(seg_ids, query_start, query_block, 0)
        scores = block_scores(query_part, key_rows, seg_query, seg_ids, score_scale)
        probs = jnp.exp(scores - log_totals[block_index][..., None])
        grad_probs = jnp.einsum(
            "qhd,khd->hqk", grad_part, value_rows, preferred_element_type=jnp.float32
        )
        inner = jnp.sum(probs * grad_probs, axis=-1, keepdims=True)
        grad_scores = (probs * (grad_probs - inner)).astype(jnp.bfloat16) * score_scale
        grad_query_part = jnp.einsum(
            "hqk,khd->qhd", grad_scores, key_rows, preferred_element_type=jnp.float32
        )
        grad_key_part = jnp.einsum(
            "hqk,qhd->khd", grad_scores, query_part, preferred_element_type=jnp.float32
        )
        grad_value_part = jnp.einsum(
            "hqk,qhd->khd",
            probs.astype(jnp.bfloat16),
            grad_part,
            preferred_element_type=jnp.float32,
        )
        grad_keys = grad_keys + grad_key_part
        grad_values = grad_values + grad_value_part
        return ((grad_keys, grad_values), grad_query_part)

    empty_grad = jnp.zeros(query_rows.shape, jnp.float32)
    (grad_keys, grad_values), grad_queries = lax.scan(
        block_step, (empty_grad, empty_grad), jnp.arange(block_count, dtype=jnp.int32)
    )
    return (grad_queries.reshape(pack_rows, heads_local, head_dim), grad_keys, grad_values)


def body(
    tokens,
    attn_gain,
    qkv_weight,
    out_weight,
    mlp_gain,
    in_weight,
    down_weight,
    seg_lengths,
    cotangent,
):
    tok_dev, model_width = tokens.shape
    pack_rows = tok_dev * lax.axis_size("tensor")
    heads_local = qkv_weight.shape[1]
    head_dim = qkv_weight.shape[2] // 3
    hidden_local = in_weight.shape[2]
    score_scale = head_dim ** (-0.5)
    query_block = min(512, pack_rows)
    qkv_full, out_full, in_full, down_full = (
        lax.all_gather(qkv_weight, "dp", axis=0, tiled=True),
        lax.all_gather(out_weight, "dp", axis=1, tiled=True),
        lax.all_gather(in_weight, "dp", axis=0, tiled=True),
        lax.all_gather(down_weight, "dp", axis=1, tiled=True),
    )
    qkv_flat = qkv_full.reshape(model_width, heads_local * 3 * head_dim)
    seg_ids, position = segment_info(seg_lengths[0], pack_rows)
    cos_table, sin_table = rotary(position, head_dim)
    row_data = tokens.astype(jnp.float32)
    normed_attn, unit_attn, inverse_attn = layer_norm(row_data, attn_gain)
    attn_input = lax.all_gather(normed_attn.astype(jnp.bfloat16), "tensor", axis=0, tiled=True)
    mixed_proj = dot_plain(attn_input, qkv_flat).reshape(pack_rows, heads_local, 3, head_dim)
    query_rows = turn(mixed_proj[:, :, 0], cos_table, sin_table).astype(jnp.bfloat16)
    key_rows = turn(mixed_proj[:, :, 1], cos_table, sin_table).astype(jnp.bfloat16)
    value_rows = mixed_proj[:, :, 2].astype(jnp.bfloat16)
    attended, log_totals = attention_forward(
        query_rows, key_rows, value_rows, seg_ids, query_block, score_scale
    )
    attended = attended.reshape(pack_rows, heads_local * head_dim).astype(jnp.bfloat16)
    residual = row_data + lax.psum_scatter(
        dot_plain(attended, out_full).astype(jnp.bfloat16),
        "tensor",
        scatter_dimension=0,
        tiled=True,
    ).astype(jnp.float32)
    normed_mlp, unit_mlp, inverse_mlp = layer_norm(residual, mlp_gain)
    mlp_input = normed_mlp.astype(jnp.bfloat16)
    mlp_rows = lax.all_gather(mlp_input, "tensor", axis=0, tiled=True)
    in_flat = in_full.reshape(model_width, -1)
    lifted = dot_plain(mlp_rows, in_flat).reshape(pack_rows, 2, hidden_local)
    act_gelu, act_slope = gelu_parts(lifted[:, 0])
    activated = (act_gelu * lifted[:, 1]).astype(jnp.bfloat16)
    layer_out = (
        residual
        + lax.psum_scatter(
            dot_plain(activated, down_full).astype(jnp.bfloat16),
            "tensor",
            scatter_dimension=0,
            tiled=True,
        ).astype(jnp.float32)
    ).astype(jnp.bfloat16)
    cotangent_rows = lax.all_gather(cotangent, "tensor", axis=0, tiled=True)
    grad_act = dot_last(cotangent_rows, down_full)
    grad_lifted = jnp.concatenate(
        [grad_act * lifted[:, 1] * act_slope, grad_act * act_gelu], axis=1
    ).astype(jnp.bfloat16)
    grad_mlp_in = lax.psum_scatter(
        dot_last(grad_lifted, in_flat).astype(jnp.bfloat16),
        "tensor",
        scatter_dimension=0,
        tiled=True,
    ).astype(jnp.float32)
    grad_in_part = dot_first(mlp_rows, grad_lifted).reshape(in_full.shape)
    grad_down_part = dot_first(activated, cotangent_rows)
    grad_resid_norm, mlp_gain_part = norm_back(grad_mlp_in, unit_mlp, inverse_mlp, mlp_gain)
    grad_residual = cotangent.astype(jnp.float32) + grad_resid_norm
    grad_branch = lax.all_gather(grad_residual.astype(jnp.bfloat16), "tensor", axis=0, tiled=True)
    grad_out_part = dot_first(attended, grad_branch)
    grad_attended = (
        dot_last(grad_branch, out_full)
        .astype(jnp.bfloat16)
        .reshape(pack_rows, heads_local, head_dim)
    )
    grad_queries, grad_keys, grad_values = attention_backward(
        query_rows,
        key_rows,
        value_rows,
        grad_attended,
        log_totals,
        seg_ids,
        query_block,
        score_scale,
    )
    grad_mixed = jnp.stack(
        [
            turn_back(grad_queries, cos_table, sin_table),
            turn_back(grad_keys, cos_table, sin_table),
            grad_values,
        ],
        axis=2,
    )
    grad_mixed = grad_mixed.reshape(pack_rows, heads_local * 3 * head_dim).astype(jnp.bfloat16)
    grad_qkv_part = dot_first(attn_input, grad_mixed).reshape(qkv_full.shape)
    grad_attn_in = lax.psum_scatter(
        dot_last(grad_mixed, qkv_flat).astype(jnp.bfloat16),
        "tensor",
        scatter_dimension=0,
        tiled=True,
    ).astype(jnp.float32)
    grad_rows_attn, attn_gain_part = norm_back(grad_attn_in, unit_attn, inverse_attn, attn_gain)
    grad_tokens = (grad_residual + grad_rows_attn).astype(jnp.bfloat16)
    qkv_grad, out_grad, in_grad, down_grad = (
        lax.psum_scatter(
            grad_qkv_part.astype(jnp.bfloat16), "dp", scatter_dimension=0, tiled=True
        ).astype(jnp.float32),
        lax.psum_scatter(
            grad_out_part.astype(jnp.bfloat16), "dp", scatter_dimension=1, tiled=True
        ).astype(jnp.float32),
        lax.psum_scatter(
            grad_in_part.astype(jnp.bfloat16), "dp", scatter_dimension=0, tiled=True
        ).astype(jnp.float32),
        lax.psum_scatter(
            grad_down_part.astype(jnp.bfloat16), "dp", scatter_dimension=1, tiled=True
        ).astype(jnp.float32),
    )
    attn_gain_grad, mlp_gain_grad = lax.psum((attn_gain_part, mlp_gain_part), ("dp", "tensor"))
    return (
        layer_out,
        grad_tokens,
        attn_gain_grad,
        qkv_grad,
        out_grad,
        mlp_gain_grad,
        in_grad,
        down_grad,
    )


def solution(mesh):
    in_specs = (
        P(("dp", "tensor"), None),
        P(),
        P("dp", "tensor", None),
        P("tensor", "dp"),
        P(),
        P("dp", None, "tensor"),
        P("tensor", "dp"),
        P("dp", None),
        P(("dp", "tensor"), None),
    )
    out_specs = (
        P(("dp", "tensor"), None),
        P(("dp", "tensor"), None),
        P(),
        P("dp", "tensor", None),
        P("tensor", "dp"),
        P(),
        P("dp", None, "tensor"),
        P("tensor", "dp"),
    )
    return jax.shard_map(body, mesh=mesh, in_specs=in_specs, out_specs=out_specs, check_vma=False)
```

profile of v0, /device:TPU:0, one launch (start us, length us, event | category | flops | bytes accessed | tf_op | source)
XLA Modules:
  0.0 726.5 jit_solution(4247788537337748045)
XLA Ops:
  11.1 2.1 fusion.107
  13.6 30.7 %all_gather.26 = bf16[256,1024]{1,0:T(8,128)(2,1)S(1)} all-gather(bf16[256,128]{1,0:T(8,128)(2,1)S(1)} %copy-done.18), channel_id=1, replica_groups=mesh['dp'=8,'tensor'=4] {'dp'}, dimensions={1}, use_global_device_ids=true | all-gather | bytes 589824 | tf_op jit(solution)/shard_map/all_gather | solution.py:189
  44.9 16.9 %all-gather.10.cloned.1.call-done = bf16[1024,4,192]{0,2,1:T(8,128)(2,1)} async-done(((bf16[128,4,192]{0,2,1:T(8,128)(2,1)}), bf16[1024,4,192]{0,2,1:T(8,128)(2,1)}) %all-gather.10.cloned.1.call-update) | async-done | bytes 1572880 | tf_op jit(solution)/shard_map/all_gather | solution.py:188
  61.8 23.0 %all-gather.8.cloned.1.call-done = bf16[1024,1024]{1,0:T(8,128)(2,1)} async-done(((bf16[256,1024]{1,0:T(8,128)(2,1)}), bf16[1024,1024]{1,0:T(8,128)(2,1)}) %all-gather.8.cloned.1.call-update) | async-done | bytes 2097168 | tf_op jit(solution)/shard_map/all_gather | solution.py:198
  84.8 3.9 fusion.89
  89.4 19.1 %while.27 = (s32[]{:T(128)}, bf16[2,512,4,64]{1,3,2,0:T(8,128)(2,1)}, f32[2,4,512]{2,1,0:T(4,128)S(1)}, s32[2]{0:T(128)S(1)}, s32[1024]{0:T(1024)S(1)}, /*index=...) while((s32[]{:T(128)}, ...), condition=%wide.region_8.9_spmd, body=%wide.region_5.8_spmd.sunk | while | flops 562558976 | bytes 33368320 | solution.py:123
  92.8 2.3 fusion.173
  95.2 3.0 fusion.174
  102.4 2.3 fusion.173
  104.7 3.0 fusion.174
  113.8 30.9 %reduce-scatter.17.cloned.1.call-done = bf16[256,1024]{1,0:T(8,128)(2,1)} async-done(((bf16[1024,1024]{1,0:T(8,128)(2,1)}), bf16[256,1024]{1,0:T(8,128)(2,1)}) %reduce-scatter.17.cloned.1.call-update) | async-done | bytes 524304 | tf_op jit(solution)/shard_map/reduce_scatter | solution.py:207
  151.3 53.2 %all-gather.14.cloned.1.call-done = bf16[1024,2,656]{0,2,1:T(8,128)(2,1)} async-done(((bf16[128,2,656]{0,2,1:T(8,128)(2,1)}), bf16[1024,2,656]{0,2,1:T(8,128)(2,1)}) %all-gather.14.cloned.1.call-update) | async-done | bytes 2686992 | tf_op jit(solution)/shard_map/all_gather | solution.py:190
  204.5 22.9 %all-gather.12.cloned.1.call-done = bf16[1024,1024]{1,0:T(8,128)(2,1)} async-done(((bf16[256,1024]{1,0:T(8,128)(2,1)}), bf16[1024,1024]{1,0:T(8,128)(2,1)}) %all-gather.12.cloned.1.call-update) | async-done | bytes 2097168 | tf_op jit(solution)/shard_map/all_gather | solution.py:215
  227.3 7.7 %fusion.86 = f32[1024,2,656]{0,2,1:T(8,128)} fusion(bf16[1024,2,656]{0,2,1:T(8,128)(2,1)} %all-gather.14.cloned.1.call-done, bf16[1024,1024]{1,0:T(8,128)(2,1)} %all-gather.12.cloned.1.call-done), kind=kOutput, calls=%fused_computation.71 | convolution fusion | flops 2751463424 | bytes 10158080 | tf_op jit(solution)/shard_map/dot_general | solution.py:15
  235.1 37.0 %all-gather.16.cloned.1.call-done = bf16[656,1024]{1,0:T(8,128)(2,1)} async-done(((bf16[656,128]{1,0:T(8,128)(2,1)}), bf16[656,1024]{1,0:T(8,128)(2,1)}) %all-gather.16.cloned.1.call-update) | async-done | bytes 1343504 | tf_op jit(solution)/shard_map/all_gather | solution.py:191
  272.1 22.9 %all-gather.18.cloned.1.call-done = bf16[1024,1024]{1,0:T(8,128)(2,1)} async-done(((bf16[256,1024]{1,0:T(8,128)(2,1)}), bf16[1024,1024]{1,0:T(8,128)(2,1)}) %all-gather.18.cloned.1.call-update) | async-done | bytes 2097168 | tf_op jit(solution)/shard_map/all_gather | solution.py:229
  295.0 7.5 %fusion.85 = (bf16[1024,656]{0,1:T(8,128)(2,1)S(1)}, bf16[1024,656]{0,1:T(8,128)(2,1)S(1)}, bf16[1024,656]{0,1:T(8,128)(2,1)}) fusion(f32[1024,2,656]{0,2,1:T(8,128)} %fusion.86, bf16[1024,1024]{1,0:T(8,128)(2,1)} %all-gather.18.cloned.1.call-done, bf16[656,1024]{1,0:T(8,128)(2,1)} %all-gather.16.cloned.1.call-done), kind=kOutput, calls=%fused_computation.67 | convolution fusion | flops 1386479616 | bytes 12845056 | tf_op jit(solution)/shard_map/dot_general | solution.py:25
  304.0 4.6 convolution_convert_fusion.1
  308.7 31.5 %reduce-scatter.21.cloned.1.call-done = bf16[256,1024]{1,0:T(8,128)(2,1)} async-done(((bf16[1024,1024]{1,0:T(8,128)(2,1)}), bf16[256,1024]{1,0:T(8,128)(2,1)}) %reduce-scatter.21.cloned.1.call-update) | async-done | bytes 524304 | tf_op jit(solution)/shard_map/reduce_scatter | solution.py:234
  341.9 2.4 fusion.124
  344.3 4.7 convolution_convert_fusion.5
  349.0 2.5 copy.38
  351.7 7.2 convolution_convert_fusion
  358.9 4.5 copy.42
  363.6 3.4 all-gather.20.cloned.1.call-done
  367.0 3.3 convolution_convert_fusion.6
  372.3 3.1 convolution_convert_fusion.7
  375.5 134.2 %while.28 = (s32[]{:T(128)}, f32[1024,4,64]{0,2,1:T(8,128)}, f32[1024,4,64]{0,2,1:T(8,128)}, f32[2,512,4,64]{1,0,3,2:T(2,128)}, s32[2]{0:T(128)S(1)}, /*index=5*...) while((s32[]{:T(128)}, f32[1024,4,64]{0,2,1:T(8,128)}, ...), condition=%wide.region_18.19_spmd.clone, body=%wide.region_16.18_spmd.clone.sunk | while | flops 1410865152 | bytes 123267416 | solution.py:163
  380.4 3.6 fusion.190
  384.1 4.5 fusion.187
  388.6 18.1 %fusion.191 = f32[1,512,4,64]{1,3,2,0:T(8,128)} fusion(bf16[1024,4,64]{0,2,1:T(8,128)(2,1)S(1)} %get-tuple-element.419, f32[4,512,1024]{2,1,0:T(8,128)} %fusion.187, f32[4,512,1024]{2,1,0:T(8,128)} %copy-done, f32[4,512]{1,0:T(4,128)S(1)} %dynamic-slice_bitcast_fusion.2, pred[512,1024]{1,0:T(8,128)(4,1)S(1)} %broadcast_compare_fusion.5), kind=kOutput, calls=%fused_computation.37.clone.1 | convolution fusion | flops 297798656 | bytes 18358272 | tf_op jit(solution)/shard_map/while/body/eval_jaxpr/hqk,khd->qhd/dot_general | solution.py:146
  406.6 23.1 %fusion.189 = f32[1024,4,64]{0,2,1:T(8,128)} fusion(f32[4,512,1024]{2,1,0:T(8,128)} %fusion.187, f32[4,512,1024]{2,1,0:T(8,128)} %copy-done, f32[4,512]{1,0:T(4,128)S(1)} %dynamic-slice_bitcast_fusion.2, pred[512,1024]{1,0:T(8,128)(4,1)S(1)} %broadcast_compare_fusion.5, f32[1024,4,64]{0,2,1:T(8,128)} %get-tuple-element.397, pred[]{:T(512)S(6)} %compare.3, ...), kind=kOutput, calls=%fused_computation.35.clone.1 | convolution fusion | flops 298322944 | bytes 36978692 | tf_op jit(solution)/shard_map/while/body/eval_jaxpr/hqk,qhd->khd/dot_general | solution.py:149
  431.4 10.3 %dynamic_update_slice.19 = f32[2,512,4,64]{1,0,3,2:T(2,128)} dynamic-update-slice(f32[2,512,4,64]{1,0,3,2:T(2,128)} %get-tuple-element.399, f32[1,512,4,64]{1,0,3,2:T(1,128)S(1)} %copy.59, s32[]{:T(128)S(6)} %copy.76, s32[]{:T(128)} %constant.35.clone.1..sunk.1, s32[]{:T(128)} %constant.35.clone.1..sunk.1, s32[]{:T(128)} %constant.35.clone.1..sunk.1) | dynamic-update-slice | bytes 1048580 | tf_op jit(solution)/shard_map/while/body/jit(dynamic_update_index_in_dim)/dynamic_update_slice | solution.py:123
  446.7 5.0 fusion.190
  451.7 4.5 fusion.187
  456.2 18.2 %fusion.191 = f32[1,512,4,64]{1,3,2,0:T(8,128)} fusion(bf16[1024,4,64]{0,2,1:T(8,128)(2,1)S(1)} %get-tuple-element.419, f32[4,512,1024]{2,1,0:T(8,128)} %fusion.187, f32[4,512,1024]{2,1,0:T(8,128)} %copy-done, f32[4,512]{1,0:T(4,128)S(1)} %dynamic-slice_bitcast_fusion.2, pred[512,1024]{1,0:T(8,128)(4,1)S(1)} %broadcast_compare_fusion.5), kind=kOutput, calls=%fused_computation.37.clone.1 | convolution fusion | flops 297798656 | bytes 18358272 | tf_op jit(solution)/shard_map/while/body/eval_jaxpr/hqk,khd->qhd/dot_general | solution.py:146
  474.4 23.2 %fusion.189 = f32[1024,4,64]{0,2,1:T(8,128)} fusion(f32[4,512,1024]{2,1,0:T(8,128)} %fusion.187, f32[4,512,1024]{2,1,0:T(8,128)} %copy-done, f32[4,512]{1,0:T(4,128)S(1)} %dynamic-slice_bitcast_fusion.2, pred[512,1024]{1,0:T(8,128)(4,1)S(1)} %broadcast_compare_fusion.5, f32[1024,4,64]{0,2,1:T(8,128)} %get-tuple-element.397, pred[]{:T(512)S(6)} %compare.3, ...), kind=kOutput, calls=%fused_computation.35.clone.1 | convolution fusion | flops 298322944 | bytes 36978692 | tf_op jit(solution)/shard_map/while/body/eval_jaxpr/hqk,qhd->khd/dot_general | solution.py:149
  499.2 10.3 %dynamic_update_slice.19 = f32[2,512,4,64]{1,0,3,2:T(2,128)} dynamic-update-slice(f32[2,512,4,64]{1,0,3,2:T(2,128)} %get-tuple-element.399, f32[1,512,4,64]{1,0,3,2:T(1,128)S(1)} %copy.59, s32[]{:T(128)S(6)} %copy.76, s32[]{:T(128)} %constant.35.clone.1..sunk.1, s32[]{:T(128)} %constant.35.clone.1..sunk.1, s32[]{:T(128)} %constant.35.clone.1..sunk.1) | dynamic-update-slice | bytes 1048580 | tf_op jit(solution)/shard_map/while/body/jit(dynamic_update_index_in_dim)/dynamic_update_slice | solution.py:123
  509.8 2.2 reshape.258
  515.5 3.0 fusion.94
  518.5 2.7 copy.40
  521.3 4.6 convolution_convert_fusion.3
  525.9 4.9 convolution_convert_fusion.4
  534.9 40.5 %reduce-scatter.27.cloned.1.call-done = bf16[128,256]{1,0:T(8,128)(2,1)} async-done(((bf16[1024,256]{1,0:T(8,128)(2,1)}), bf16[128,256]{1,0:T(8,128)(2,1)}) %reduce-scatter.27.cloned.1.call-update) | async-done | bytes 65552
  577.1 65.6 %reduce-scatter.25.cloned.1.call-done = bf16[128,768]{1,0:T(8,128)(2,1)} async-done(((bf16[1024,768]{1,0:T(8,128)(2,1)}), bf16[128,768]{1,0:T(8,128)(2,1)}) %reduce-scatter.25.cloned.1.call-update) | async-done | bytes 196624
  644.6 31.1 %reduce-scatter.23.cloned.1.call-done = bf16[256,1024]{1,0:T(8,128)(2,1)} async-done(((bf16[1024,1024]{1,0:T(8,128)(2,1)}), bf16[256,1024]{1,0:T(8,128)(2,1)}) %reduce-scatter.23.cloned.1.call-update) | async-done | bytes 524304 | tf_op jit(solution)/shard_map/reduce_scatter | solution.py:271
  677.2 39.4 %all-reduce = (f32[1024]{0:T(1024)}, f32[1024]{0:T(1024)}) all-reduce(f32[1024]{0:T(1024)S(1)} %get-tuple-element.153, f32[1024]{0:T(1024)S(1)} %get-tuple-element.151), channel_id=1, replica_groups=mesh['dp'=8,'tensor'=4] {'dp','tensor'}, use_global_device_ids=true, to_apply=%region_23.24 | all-reduce | flops 2048 | bytes 16384 | tf_op jit(solution)/shard_map/psum | solution.py:293
  716.7 3.0 fusion.111
  (171 shorter events, 50.4 us)
Async XLA Ops:
  7.2 6.2 copy-start.25
  7.2 6.5 copy-start.18
  7.2 54.6 %all-gather.10.cloned.1.call-start = ((), (), s32[]{:S(2)}) async-start(), calls=%async_computation.9 | async-start | bytes 1769472 | tf_op jit(solution)/shard_map/all_gather | solution.py:188
  7.9 76.8 %all-gather.8.cloned.1.call-start = ((), (), s32[]{:S(2)}) async-start(), calls=%async_computation.8 | async-start | bytes 2621440 | tf_op jit(solution)/shard_map/all_gather | solution.py:198
  9.2 1.4 copy-start.21
  13.2 131.5 %reduce-scatter.17.cloned.1.call-start = ((), (), s32[]{:S(2)}) async-start(), calls=%async_computation.10 | async-start | bytes 2621440 | tf_op jit(solution)/shard_map/reduce_scatter | solution.py:207
  44.4 65.9 %copy-start.7 = (bf16[256,1024]{1,0:T(8,128)(2,1)}, bf16[256,1024]{1,0:T(8,128)(2,1)S(1)}, u32[]{:S(2)}) copy-start(bf16[256,1024]{1,0:T(8,128)(2,1)S(1)} %all_gather.26) | copy-start | bytes 1572868
  44.9 44.1 %copy-start.12 = (f32[1024,32]{0,1:T(8,128)}, f32[1024,32]{0,1:T(8,128)S(1)}, u32[]{:S(2)}) copy-start(f32[1024,32]{0,1:T(8,128)S(1)} %get-tuple-element.220) | copy-start | bytes 393220
  44.9 44.1 %copy-start.14 = (f32[1024,32]{0,1:T(8,128)}, f32[1024,32]{0,1:T(8,128)S(1)}, u32[]{:S(2)}) copy-start(f32[1024,32]{0,1:T(8,128)S(1)} %get-tuple-element.221) | copy-start | bytes 393220
  92.8 2.3 copy-start.16
  98.2 0.8 copy-start.17
  102.4 2.3 copy-start.16
  107.8 0.8 copy-start.17
  110.2 0.8 copy-start.9
  111.0 33.7 %copy-start.1 = (bf16[256,1024]{1,0:T(8,128)(2,1)S(1)}, bf16[256,1024]{1,0:T(8,128)(2,1)}, u32[]{:S(2)}) copy-start(bf16[256,1024]{1,0:T(8,128)(2,1)} %param.13) | copy-start | bytes 1572868
  113.1 34.2 %copy-start.19 = (f32[1024]{0:T(1024)S(1)}, f32[1024]{0:T(1024)}, u32[]{:S(2)}) copy-start(f32[1024]{0:T(1024)} %param.17) | copy-start | bytes 12292
  113.1 91.3 %all-gather.14.cloned.1.call-start = ((), (), s32[]{:S(2)}) async-start(), calls=%async_computation.12 | async-start | bytes 3022848 | tf_op jit(solution)/shard_map/all_gather | solution.py:190
  113.7 113.6 %all-gather.12.cloned.1.call-start = ((), (), s32[]{:S(2)}) async-start(), calls=%async_computation.11 | async-start | bytes 2621440 | tf_op jit(solution)/shard_map/all_gather | solution.py:215
  149.4 122.6 %all-gather.16.cloned.1.call-start = ((), (), s32[]{:S(2)}) async-start(), calls=%async_computation.13 | async-start | bytes 1511424 | tf_op jit(solution)/shard_map/all_gather | solution.py:191
  150.0 145.0 %all-gather.18.cloned.1.call-start = ((), (), s32[]{:S(2)}) async-start(), calls=%async_computation.15 | async-start | bytes 2621440 | tf_op jit(solution)/shard_map/all_gather | solution.py:229
  150.8 189.5 %reduce-scatter.21.cloned.1.call-start = ((), (), s32[]{:S(2)}) async-start(), calls=%async_computation.16 | async-start | bytes 2621440 | tf_op jit(solution)/shard_map/reduce_scatter | solution.py:234
  295.0 9.0 %copy-start.26 = (bf16[1024,2,656]{0,2,1:T(8,128)(2,1)S(1)}, bf16[1024,2,656]{0,2,1:T(8,128)(2,1)}, u32[]{:S(2)}) copy-start(bf16[1024,2,656]{0,2,1:T(8,128)(2,1)} %all-gather.14.cloned.1.call-done) | copy-start | bytes 8060932
  302.5 1.1 copy-start.28
  302.5 1.5 copy-start.29
  304.0 36.3 %copy-start.2 = (bf16[256,1024]{1,0:T(8,128)(2,1)S(1)}, bf16[256,1024]{1,0:T(8,128)(2,1)}, u32[]{:S(2)}) copy-start(bf16[256,1024]{1,0:T(8,128)(2,1)} %reduce-scatter.17.cloned.1.call-done) | copy-start | bytes 1572868
  308.6 33.3 %copy-start.4 = (bf16[256,1024]{1,0:T(8,128)(2,1)S(1)}, bf16[256,1024]{1,0:T(8,128)(2,1)}, u32[]{:S(2)}) copy-start(bf16[256,1024]{1,0:T(8,128)(2,1)} %param.21) | copy-start | bytes 1572868
  308.6 58.4 %all-gather.20.cloned.1.call-start = ((), (), s32[]{:S(2)}) async-start(), calls=%async_computation.17 | async-start | bytes 2621440 | tf_op jit(solution)/shard_map/all_gather | solution.py:244
  344.3 186.6 %reduce-scatter.31.cloned.1.call-start = ((), (), s32[]{:S(2)}) async-start(), calls=%async_computation.22 | async-start | bytes 1769472
  351.6 181.2 %reduce-scatter.29.cloned.1.call-start = ((), (), s32[]{:S(2)}) async-start(), calls=%async_computation.21 | async-start | bytes 3244032
  363.4 8.9 %copy-start.8 = (bf16[256,1024]{1,0:T(8,128)(2,1)S(1)}, bf16[256,1024]{1,0:T(8,128)(2,1)}, u32[]{:S(2)}) copy-start(bf16[256,1024]{1,0:T(8,128)(2,1)} %copy-done.7) | copy-start | bytes 1572868
  363.4 212.0 %reduce-scatter.27.cloned.1.call-start = ((), (), s32[]{:S(2)}) async-start(), calls=%async_computation.20 | async-start | bytes 589824
  379.1 1.3 copy-start.6
  380.4 3.6 copy-start
  445.3 1.3 copy-start.6
  446.7 5.0 copy-start
  509.7 2.3 copy-start.13
  509.7 2.3 copy-start.15
  511.9 130.8 %reduce-scatter.25.cloned.1.call-start = ((), (), s32[]{:S(2)}) async-start(), calls=%async_computation.19 | async-start | bytes 1769472
  513.6 1.9 copy-start.27
  515.3 3.2 copy-start.10
  518.5 2.8 copy-start.11
  521.2 154.4 %reduce-scatter.23.cloned.1.call-start = ((), (), s32[]{:S(2)}) async-start(), calls=%async_computation.18 | async-start | bytes 2621440 | tf_op jit(solution)/shard_map/reduce_scatter | solution.py:271
  525.9 190.8 %reduce-scatter.19.cloned.1.call-start = ((), (), s32[]{:S(2)}) async-start(), calls=%async_computation.14 | async-start | bytes 2621440 | tf_op jit(solution)/shard_map/reduce_scatter | solution.py:222
  530.8 144.8 %copy-start.20 = (f32[1024]{0:T(1024)S(1)}, f32[1024]{0:T(1024)}, u32[]{:S(2)}) copy-start(f32[1024]{0:T(1024)} %param.14) | copy-start | bytes 12292
  530.8 144.8 %copy-start.22 = (f32[256]{0:T(256)S(1)}, f32[256]{0:T(256)}, u32[]{:S(2)}) copy-start(f32[256]{0:T(256)} %copy-done.21) | copy-start | bytes 3076
  530.8 144.8 %copy-start.24 = (f32[256]{0:T(256)S(1)}, f32[256]{0:T(256)}, u32[]{:S(2)}) copy-start(f32[256]{0:T(256)} %copy-done.23) | copy-start | bytes 3076
  530.9 185.8 %copy-start.3 = (bf16[256,1024]{1,0:T(8,128)(2,1)S(1)}, bf16[256,1024]{1,0:T(8,128)(2,1)}, u32[]{:S(2)}) copy-start(bf16[256,1024]{1,0:T(8,128)(2,1)} %reduce-scatter.21.cloned.1.call-done) | copy-start | bytes 1572868
  530.9 185.8 %copy-start.5 = (bf16[256,1024]{1,0:T(8,128)(2,1)S(1)}, bf16[256,1024]{1,0:T(8,128)(2,1)}, u32[]{:S(2)}) copy-start(bf16[256,1024]{1,0:T(8,128)(2,1)} %param.21) | copy-start | bytes 1572868
  (1 other events, 0.6 us)
Sparse Core Ops, SparseCore 0:
  10.1 51.6 all-gather.9
  63.9 20.7 all-gather.7
  113.2 31.4 reduce-scatter.16
  146.8 57.6 all-gather.13
  206.5 20.7 all-gather.11
  229.4 42.5 all-gather.15
  273.7 21.2 all-gather.17
  308.7 31.4 reduce-scatter.20
  344.4 22.5 all-gather.19
  370.3 64.9 reduce-scatter.30
  439.3 70.6 reduce-scatter.28
  514.1 61.2 reduce-scatter.26
  578.9 63.7 reduce-scatter.24
  645.2 30.3 reduce-scatter.22
  678.0 31.4 reduce-scatter.18
where the time goes:
time: 736 us; the launch traced here: 726 us
  waiting for transfers between devices  382 us (52%)
  matrix products  169 us (23%)
  blocking collectives  70.2 us (10%)
  local copies, waits for them, and re-layouts  51.6 us (7%)
  other arithmetic  31.6 us (4%)
  between operations  14.6 us (2%)
    unnamed x19, waiting for transfers between devices  109 us
    all_gather x1, waiting for transfers between devices, body(): lax.all_gather(in_weight, 'dp', axis=0, tiled=True)  53.2 us
    dot_general x2, matrix products, block_step(): jnp.einsum('hqk,qhd->khd', grad_scores, query_part, preferred_element_typ...  46.3 us
    psum x1, blocking collectives, body(): lax.psum((attn_gain_part, mlp_gain_part), ('dp', 'tensor'))  39.4 us
    all_gather x1, waiting for transfers between devices, body(): lax.all_gather(down_weight, 'dp', axis=1, tiled=True)  37 us
    dot_general x2, matrix products, block_step(): jnp.einsum('hqk,khd->qhd', grad_scores, key_rows, preferred_element_type=...  36.2 us
    reduce_scatter x1, waiting for transfers between devices, body(): lax.psum_scatter(dot_last(grad_lifted, in_flat).astype(jnp.bfloat16), 'te...  31.5 us
    reduce_scatter x1, waiting for transfers between devices, body(): lax.psum_scatter(dot_last(grad_mixed, qkv_flat).astype(jnp.bfloat16), 'te...  31.1 us
  transfers between devices with their start and end apart: 15, of which 12 were waited for; matrix products, arithmetic and copies ran while one was open for 28% of the time, Pallas kernels for 0%

commit v1 on v0

--- a/solution.py
+++ b/solution.py
@@ -9,6 +9,17 @@
 HALF_ROOT = 0.7071067811865476
 INV_ROOT_TAU = 0.3989422804014327
 MASKED_SCORE = -1e30
+
+
+def turned_line(block, axis, dim):
+    size = lax.axis_size(axis)
+    forward = [(i, (i + 1) % size) for i in range(size)]
+    parts = [block]
+    for hop in range(1, size):
+        parts = [lax.ppermute(parts[0], axis, forward), *parts]
+    full = jnp.concatenate(parts, axis=dim)
+    shift = (lax.axis_index(axis) + 1) * parts[-1].shape[dim]
+    return jnp.roll(full, shift, axis=dim)
 
 
 def dot_plain(left, right):
@@ -212,7 +223,7 @@
     ).astype(jnp.float32)
     normed_mlp, unit_mlp, inverse_mlp = layer_norm(residual, mlp_gain)
     mlp_input = normed_mlp.astype(jnp.bfloat16)
-    mlp_rows = lax.all_gather(mlp_input, "tensor", axis=0, tiled=True)
+    mlp_rows = turned_line(mlp_input, "tensor", 0)
     in_flat = in_full.reshape(model_width, -1)
     lifted = dot_plain(mlp_rows, in_flat).reshape(pack_rows, 2, hidden_local)
     act_gelu, act_slope = gelu_parts(lifted[:, 0])

time: 736 us -> 713 us (0.969)
  waiting for transfers between devices: 382 us -> 345 us
  local copies, waits for them, and re-layouts: 51.6 us -> 62.6 us
    all_gather x1, waiting for transfers between devices: 53.2 us -> 18.1 us  [body(): lax.all_gather(in_weight, 'dp', axis=0, tiled=True)]
    ppermute x0 -> x3, waiting for transfers between devices: none -> 26.1 us  [turned_line(): parts = [lax.ppermute(parts[0], axis, forward), *parts]]
    all_gather x1 -> x0, waiting for transfers between devices: 22.9 us -> none  [body(): mlp_rows = lax.all_gather(mlp_input, 'tensor', axis=0, tiled=True)]
    unnamed x61 -> x64, local copies, waits for them, and re-layouts: 19.4 us -> 29.5 us
    unnamed x19 -> x18, waiting for transfers between devices: 109 us -> 108 us
  transfers between devices with their start and end apart: 15 -> 17, of which waited for: 12 -> 14; matrix products, arithmetic and copies ran while one was open for 28% -> 31% of each run, Pallas kernels for 0% -> 0%
where the time goes in v1:
time: 713 us; the launch traced here: 702 us
  waiting for transfers between devices  345 us (48%)
  matrix products  169 us (24%)
  blocking collectives  71 us (10%)
  local copies, waits for them, and re-layouts  62.6 us (9%)
  other arithmetic  32.1 us (5%)
  between operations  14.6 us (2%)
    unnamed x18, waiting for transfers between devices  108 us
    dot_general x2, matrix products, block_step(): jnp.einsum('hqk,qhd->khd', grad_scores, query_part, preferred_element_typ...  46.3 us
    psum x1, blocking collectives, body(): lax.psum((attn_gain_part, mlp_gain_part), ('dp', 'tensor'))  39.4 us
    dot_general x2, matrix products, block_step(): jnp.einsum('hqk,khd->qhd', grad_scores, key_rows, preferred_element_type=...  36.3 us
    all_gather x1, waiting for transfers between devices, body(): lax.all_gather(down_weight, 'dp', axis=1, tiled=True)  35.2 us
    all_gather x1, blocking collectives, body(): lax.all_gather(out_weight, 'dp', axis=1, tiled=True)  31.6 us
    reduce_scatter x1, waiting for transfers between devices, body(): lax.psum_scatter(dot_last(grad_lifted, in_flat).astype(jnp.bfloat16), 'te...  31.5 us
    reduce_scatter x1, waiting for transfers between devices, body(): lax.psum_scatter(dot_last(grad_mixed, qkv_flat).astype(jnp.bfloat16), 'te...  31.2 us
  transfers between devices with their start and end apart: 17, of which 14 were waited for; matrix products, arithmetic and copies ran while one was open for 31% of the time, Pallas kernels for 0%

profile of v1, /device:TPU:0, one launch (start us, length us, event | category | flops | bytes accessed | tf_op | source)
XLA Modules:
  0.0 702.3 jit_solution(13707431006040212838)
XLA Ops:
  14.9 31.6 %all_gather.23 = bf16[256,1024]{1,0:T(8,128)(2,1)S(1)} all-gather(bf16[256,128]{1,0:T(8,128)(2,1)} %param.16), channel_id=1, replica_groups=mesh['dp'=8,'tensor'=4] {'dp'}, dimensions={1}, use_global_device_ids=true | all-gather | bytes 589824 | tf_op jit(solution)/shard_map/all_gather | solution.py:200
  47.1 14.4 %all-gather.9.cloned.1.call-done = bf16[1024,4,192]{0,2,1:T(8,128)(2,1)} async-done(((bf16[128,4,192]{0,2,1:T(8,128)(2,1)}), bf16[1024,4,192]{0,2,1:T(8,128)(2,1)}) %all-gather.9.cloned.1.call-update) | async-done | bytes 1572880 | tf_op jit(solution)/shard_map/all_gather | solution.py:199
  61.5 23.4 %all-gather.7.cloned.1.call-done = bf16[1024,1024]{1,0:T(8,128)(2,1)} async-done(((bf16[256,1024]{1,0:T(8,128)(2,1)}), bf16[1024,1024]{1,0:T(8,128)(2,1)}) %all-gather.7.cloned.1.call-update) | async-done | bytes 2097168 | tf_op jit(solution)/shard_map/all_gather | solution.py:209
  84.9 3.9 fusion.89
  89.5 19.1 %while.27 = (s32[]{:T(128)}, bf16[2,512,4,64]{1,3,2,0:T(8,128)(2,1)}, f32[2,4,512]{2,1,0:T(4,128)S(1)}, s32[2]{0:T(128)S(1)}, s32[1024]{0:T(1024)S(1)}, /*index=...) while((s32[]{:T(128)}, ...), condition=%wide.region_8.9_spmd, body=%wide.region_5.8_spmd.sunk | while | flops 562558976 | bytes 33368320 | solution.py:134
  92.9 2.3 fusion.176
  95.3 3.0 fusion.177
  102.5 2.3 fusion.176
  104.8 3.0 fusion.177
  114.5 30.4 %reduce-scatter.17.cloned.1.call-done = bf16[256,1024]{1,0:T(8,128)(2,1)} async-done(((bf16[1024,1024]{1,0:T(8,128)(2,1)}), bf16[256,1024]{1,0:T(8,128)(2,1)}) %reduce-scatter.17.cloned.1.call-update) | async-done | bytes 524304 | tf_op jit(solution)/shard_map/reduce_scatter | solution.py:218
  148.9 8.5 %collective-permute-done = bf16[256,1024]{1,0:T(8,128)(2,1)S(1)} collective-permute-done((bf16[256,1024]{1,0:T(8,128)(2,1)S(1)}, bf16[256,1024]{1,0:T(8,128)(2,1)S(1)}, u32[]{:S(2)}, u32[]{:S(2)}) %collective-permute-start) | collective-permute-done | bytes 524320 | tf_op jit(solution)/shard_map/ppermute | solution.py:19
  157.5 8.7 %collective-permute-done.1 = bf16[256,1024]{1,0:T(8,128)(2,1)} collective-permute-done((bf16[256,1024]{1,0:T(8,128)(2,1)S(1)}, bf16[256,1024]{1,0:T(8,128)(2,1)}, u32[]{:S(2)}, u32[]{:S(2)}) %collective-permute-start.1) | collective-permute-done | bytes 524320 | tf_op jit(solution)/shard_map/ppermute | solution.py:19
  166.6 8.9 %collective-permute-done.2 = bf16[256,1024]{1,0:T(8,128)(2,1)} collective-permute-done((bf16[256,1024]{1,0:T(8,128)(2,1)}, bf16[256,1024]{1,0:T(8,128)(2,1)}, u32[]{:S(2)}, u32[]{:S(2)}) %collective-permute-start.2) | collective-permute-done | bytes 524320 | tf_op jit(solution)/shard_map/ppermute | solution.py:19
  186.5 18.1 %all-gather.11.cloned.1.call-done = bf16[1024,2,656]{0,2,1:T(8,128)(2,1)} async-done(((bf16[128,2,656]{0,2,1:T(8,128)(2,1)}), bf16[1024,2,656]{0,2,1:T(8,128)(2,1)}) %all-gather.11.cloned.1.call-update) | async-done | bytes 2686992 | tf_op jit(solution)/shard_map/all_gather | solution.py:201
  204.7 7.7 %fusion.86 = f32[1024,2,656]{0,2,1:T(8,128)} fusion(bf16[1024,2,656]{0,2,1:T(8,128)(2,1)} %all-gather.11.cloned.1.call-done, bf16[2048,1024]{1,0:T(8,128)(2,1)} %constant_dynamic-update-slice_fusion, s32[]{:T(128)S(6)} %select_n.38), kind=kOutput, calls=%fused_computation.71 | convolution fusion | flops 2751463424 | bytes 10158084 | tf_op jit(solution)/shard_map/dot_general | solution.py:26
  212.4 35.2 %all-gather.13.cloned.1.call-done = bf16[656,1024]{1,0:T(8,128)(2,1)} async-done(((bf16[656,128]{1,0:T(8,128)(2,1)}), bf16[656,1024]{1,0:T(8,128)(2,1)}) %all-gather.13.cloned.1.call-update) | async-done | bytes 1343504 | tf_op jit(solution)/shard_map/all_gather | solution.py:202
  247.6 22.7 %all-gather.15.cloned.1.call-done = bf16[1024,1024]{1,0:T(8,128)(2,1)} async-done(((bf16[256,1024]{1,0:T(8,128)(2,1)}), bf16[1024,1024]{1,0:T(8,128)(2,1)}) %all-gather.15.cloned.1.call-update) | async-done | bytes 2097168 | tf_op jit(solution)/shard_map/all_gather | solution.py:240
  270.3 7.5 %fusion.85 = (bf16[1024,656]{0,1:T(8,128)(2,1)S(1)}, bf16[1024,656]{0,1:T(8,128)(2,1)S(1)}, bf16[1024,656]{0,1:T(8,128)(2,1)}) fusion(f32[1024,2,656]{0,2,1:T(8,128)} %fusion.86, bf16[1024,1024]{1,0:T(8,128)(2,1)} %all-gather.15.cloned.1.call-done, bf16[656,1024]{1,0:T(8,128)(2,1)} %all-gather.13.cloned.1.call-done), kind=kOutput, calls=%fused_computation.67 | convolution fusion | flops 1386479616 | bytes 12845056 | tf_op jit(solution)/shard_map/dot_general | solution.py:36
  279.3 4.7 convolution_convert_fusion.1
  284.0 31.5 %reduce-scatter.21.cloned.1.call-done = bf16[256,1024]{1,0:T(8,128)(2,1)} async-done(((bf16[1024,1024]{1,0:T(8,128)(2,1)}), bf16[256,1024]{1,0:T(8,128)(2,1)}) %reduce-scatter.21.cloned.1.call-update) | async-done | bytes 524304 | tf_op jit(solution)/shard_map/reduce_scatter | solution.py:245
  317.2 2.4 fusion.128
  319.7 4.7 convolution_convert_fusion.5
  324.4 2.5 copy.38
  327.0 7.2 %convolution_convert_fusion = bf16[1024,1312]{0,1:T(8,128)(2,1)} fusion(bf16[2048,1024]{1,0:T(8,128)(2,1)} %constant_dynamic-update-slice_fusion, s32[]{:T(128)S(6)} %select_n.38, bf16[1024,656]{0,1:T(8,128)(2,1)} %copy-done.27, bf16[1024,656]{0,1:T(8,128)(2,1)} %copy-done.26), kind=kOutput, calls=%fused_computation.61 | convolution fusion | flops 2758180864 | bytes 7471108 | tf_op jit(solution)/shard_map/dot_general | solution.py:30
  334.2 4.5 copy.42
  338.8 3.6 all-gather.17.cloned.1.call-done
  342.4 3.3 convolution_convert_fusion.6
  347.7 3.1 convolution_convert_fusion.7
  350.8 134.4 %while.28 = (s32[]{:T(128)}, f32[1024,4,64]{0,2,1:T(8,128)}, f32[1024,4,64]{0,2,1:T(8,128)}, f32[2,512,4,64]{1,0,3,2:T(2,128)}, s32[2]{0:T(128)S(1)}, /*index=5*...) while((s32[]{:T(128)}, f32[1024,4,64]{0,2,1:T(8,128)}, ...), condition=%wide.region_18.19_spmd.clone, body=%wide.region_16.18_spmd.clone.sunk | while | flops 1410865152 | bytes 123267416 | solution.py:174
  356.0 3.6 fusion.193
  359.6 4.5 fusion.190
  364.1 18.1 %fusion.194 = f32[1,512,4,64]{1,3,2,0:T(8,128)} fusion(bf16[1024,4,64]{0,2,1:T(8,128)(2,1)S(1)} %get-tuple-element.419, f32[4,512,1024]{2,1,0:T(8,128)} %fusion.190, f32[4,512,1024]{2,1,0:T(8,128)} %copy-done, f32[4,512]{1,0:T(4,128)S(1)} %dynamic-slice_bitcast_fusion.2, pred[512,1024]{1,0:T(8,128)(4,1)S(1)} %broadcast_compare_fusion.5), kind=kOutput, calls=%fused_computation.37.clone.1 | convolution fusion | flops 297798656 | bytes 18358272 | tf_op jit(solution)/shard_map/while/body/eval_jaxpr/hqk,khd->qhd/dot_general | solution.py:157
  382.2 23.1 %fusion.192 = f32[1024,4,64]{0,2,1:T(8,128)} fusion(f32[4,512,1024]{2,1,0:T(8,128)} %fusion.190, f32[4,512,1024]{2,1,0:T(8,128)} %copy-done, f32[4,512]{1,0:T(4,128)S(1)} %dynamic-slice_bitcast_fusion.2, pred[512,1024]{1,0:T(8,128)(4,1)S(1)} %broadcast_compare_fusion.5, f32[1024,4,64]{0,2,1:T(8,128)} %get-tuple-element.397, pred[]{:T(512)S(6)} %compare.4, ...), kind=kOutput, calls=%fused_computation.35.clone.1 | convolution fusion | flops 298322944 | bytes 36978692 | tf_op jit(solution)/shard_map/while/body/eval_jaxpr/hqk,qhd->khd/dot_general | solution.py:160
  406.9 10.3 %dynamic_update_slice.19 = f32[2,512,4,64]{1,0,3,2:T(2,128)} dynamic-update-slice(f32[2,512,4,64]{1,0,3,2:T(2,128)} %get-tuple-element.399, f32[1,512,4,64]{1,0,3,2:T(1,128)S(1)} %copy.59, s32[]{:T(128)S(6)} %copy.83, s32[]{:T(128)} %constant.91.clone.1..sunk.1, s32[]{:T(128)} %constant.91.clone.1..sunk.1, s32[]{:T(128)} %constant.91.clone.1..sunk.1) | dynamic-update-slice | bytes 1048580 | tf_op jit(solution)/shard_map/while/body/jit(dynamic_update_index_in_dim)/dynamic_update_slice | solution.py:134
  422.2 5.0 fusion.193
  427.2 4.5 fusion.190
  431.7 18.2 %fusion.194 = f32[1,512,4,64]{1,3,2,0:T(8,128)} fusion(bf16[1024,4,64]{0,2,1:T(8,128)(2,1)S(1)} %get-tuple-element.419, f32[4,512,1024]{2,1,0:T(8,128)} %fusion.190, f32[4,512,1024]{2,1,0:T(8,128)} %copy-done, f32[4,512]{1,0:T(4,128)S(1)} %dynamic-slice_bitcast_fusion.2, pred[512,1024]{1,0:T(8,128)(4,1)S(1)} %broadcast_compare_fusion.5), kind=kOutput, calls=%fused_computation.37.clone.1 | convolution fusion | flops 297798656 | bytes 18358272 | tf_op jit(solution)/shard_map/while/body/eval_jaxpr/hqk,khd->qhd/dot_general | solution.py:157
  449.9 23.2 %fusion.192 = f32[1024,4,64]{0,2,1:T(8,128)} fusion(f32[4,512,1024]{2,1,0:T(8,128)} %fusion.190, f32[4,512,1024]{2,1,0:T(8,128)} %copy-done, f32[4,512]{1,0:T(4,128)S(1)} %dynamic-slice_bitcast_fusion.2, pred[512,1024]{1,0:T(8,128)(4,1)S(1)} %broadcast_compare_fusion.5, f32[1024,4,64]{0,2,1:T(8,128)} %get-tuple-element.397, pred[]{:T(512)S(6)} %compare.4, ...), kind=kOutput, calls=%fused_computation.35.clone.1 | convolution fusion | flops 298322944 | bytes 36978692 | tf_op jit(solution)/shard_map/while/body/eval_jaxpr/hqk,qhd->khd/dot_general | solution.py:160
  474.7 10.3 %dynamic_update_slice.19 = f32[2,512,4,64]{1,0,3,2:T(2,128)} dynamic-update-slice(f32[2,512,4,64]{1,0,3,2:T(2,128)} %get-tuple-element.399, f32[1,512,4,64]{1,0,3,2:T(1,128)S(1)} %copy.59, s32[]{:T(128)S(6)} %copy.83, s32[]{:T(128)} %constant.91.clone.1..sunk.1, s32[]{:T(128)} %constant.91.clone.1..sunk.1, s32[]{:T(128)} %constant.91.clone.1..sunk.1) | dynamic-update-slice | bytes 1048580 | tf_op jit(solution)/shard_map/while/body/jit(dynamic_update_index_in_dim)/dynamic_update_slice | solution.py:134
  491.0 3.0 fusion.96
  493.9 2.7 copy.40
  496.7 4.6 convolution_convert_fusion.3
  501.4 4.9 convolution_convert_fusion.4
  510.4 40.8 %reduce-scatter.27.cloned.1.call-done = bf16[128,256]{1,0:T(8,128)(2,1)} async-done(((bf16[1024,256]{1,0:T(8,128)(2,1)}), bf16[128,256]{1,0:T(8,128)(2,1)}) %reduce-scatter.27.cloned.1.call-update) | async-done | bytes 65552
  552.9 65.6 %reduce-scatter.25.cloned.1.call-done = bf16[128,768]{1,0:T(8,128)(2,1)} async-done(((bf16[1024,768]{1,0:T(8,128)(2,1)}), bf16[128,768]{1,0:T(8,128)(2,1)}) %reduce-scatter.25.cloned.1.call-update) | async-done | bytes 196624
  620.3 31.2 %reduce-scatter.23.cloned.1.call-done = bf16[256,1024]{1,0:T(8,128)(2,1)} async-done(((bf16[1024,1024]{1,0:T(8,128)(2,1)}), bf16[256,1024]{1,0:T(8,128)(2,1)}) %reduce-scatter.23.cloned.1.call-update) | async-done | bytes 524304 | tf_op jit(solution)/shard_map/reduce_scatter | solution.py:282
  653.1 39.4 %all-reduce = (f32[1024]{0:T(1024)}, f32[1024]{0:T(1024)}) all-reduce(f32[1024]{0:T(1024)S(1)} %get-tuple-element.153, f32[1024]{0:T(1024)S(1)} %get-tuple-element.151), channel_id=1, replica_groups=mesh['dp'=8,'tensor'=4] {'dp','tensor'}, use_global_device_ids=true, to_apply=%region_23.24 | all-reduce | flops 2048 | bytes 16384 | tf_op jit(solution)/shard_map/psum | solution.py:304
  692.6 3.0 fusion.113
  (178 shorter events, 65.3 us)
Async XLA Ops:
  7.2 54.3 %all-gather.9.cloned.1.call-start = ((), (), s32[]{:S(2)}) async-start(), calls=%async_computation.9 | async-start | bytes 1769472 | tf_op jit(solution)/shard_map/all_gather | solution.py:199
  7.9 77.0 %all-gather.7.cloned.1.call-start = ((), (), s32[]{:S(2)}) async-start(), calls=%async_computation.8 | async-start | bytes 2621440 | tf_op jit(solution)/shard_map/all_gather | solution.py:209
  9.1 1.4 copy-start.20
  13.2 131.7 %reduce-scatter.17.cloned.1.call-start = ((), (), s32[]{:S(2)}) async-start(), calls=%async_computation.10 | async-start | bytes 2621440 | tf_op jit(solution)/shard_map/reduce_scatter | solution.py:218
  46.5 63.9 %copy-start.7 = (bf16[256,1024]{1,0:T(8,128)(2,1)}, bf16[256,1024]{1,0:T(8,128)(2,1)S(1)}, u32[]{:S(2)}) copy-start(bf16[256,1024]{1,0:T(8,128)(2,1)S(1)} %all_gather.23) | copy-start | bytes 1572868
  47.0 42.0 %copy-start.12 = (f32[1024,32]{0,1:T(8,128)}, f32[1024,32]{0,1:T(8,128)S(1)}, u32[]{:S(2)}) copy-start(f32[1024,32]{0,1:T(8,128)S(1)} %get-tuple-element.220) | copy-start | bytes 393220
  47.1 42.0 %copy-start.14 = (f32[1024,32]{0,1:T(8,128)}, f32[1024,32]{0,1:T(8,128)S(1)}, u32[]{:S(2)}) copy-start(f32[1024,32]{0,1:T(8,128)S(1)} %get-tuple-element.221) | copy-start | bytes 393220
  92.9 2.3 copy-start.16
  98.3 0.8 copy-start.17
  102.5 2.3 copy-start.16
  107.8 0.8 copy-start.17
  108.6 36.3 %copy-start.1 = (bf16[256,1024]{1,0:T(8,128)(2,1)S(1)}, bf16[256,1024]{1,0:T(8,128)(2,1)}, u32[]{:S(2)}) copy-start(bf16[256,1024]{1,0:T(8,128)(2,1)} %param.13) | copy-start | bytes 1572868
  110.3 37.2 %copy-start.18 = (f32[1024]{0:T(1024)S(1)}, f32[1024]{0:T(1024)}, u32[]{:S(2)}) copy-start(f32[1024]{0:T(1024)} %param.17) | copy-start | bytes 12292
  110.4 0.8 copy-start.9
  113.3 91.4 %all-gather.11.cloned.1.call-start = ((), (), s32[]{:S(2)}) async-start(), calls=%async_computation.11 | async-start | bytes 3022848 | tf_op jit(solution)/shard_map/all_gather | solution.py:201
  113.9 133.7 %all-gather.13.cloned.1.call-start = ((), (), s32[]{:S(2)}) async-start(), calls=%async_computation.12 | async-start | bytes 1511424 | tf_op jit(solution)/shard_map/all_gather | solution.py:202
  114.5 155.8 %all-gather.15.cloned.1.call-start = ((), (), s32[]{:S(2)}) async-start(), calls=%async_computation.14 | async-start | bytes 2621440 | tf_op jit(solution)/shard_map/all_gather | solution.py:240
  148.8 8.7 %collective-permute-start = (bf16[256,1024]{1,0:T(8,128)(2,1)S(1)}, bf16[256,1024]{1,0:T(8,128)(2,1)S(1)}, u32[]{:S(2)}, u32[]{:S(2)}) collective-permute-start(bf16[256,1024]{1,0:T(8,128)(2,1)S(1)} %multiply_convert_fusion.3), channel_id=1, source_target_pairs={{0,1},{1,2},{2,3},{3,0},{4,5},{5,6},{6,7},{7,4},{8,9},{9,10},{10,1... | collective-permute-start | bytes 1572872 | tf_op jit(solution)/shard_map/ppermute | solution.py:19
  148.9 166.7 %reduce-scatter.21.cloned.1.call-start = ((), (), s32[]{:S(2)}) async-start(), calls=%async_computation.15 | async-start | bytes 2621440 | tf_op jit(solution)/shard_map/reduce_scatter | solution.py:245
  157.5 8.7 %collective-permute-start.1 = (bf16[256,1024]{1,0:T(8,128)(2,1)S(1)}, bf16[256,1024]{1,0:T(8,128)(2,1)}, u32[]{:S(2)}, u32[]{:S(2)}) collective-permute-start(bf16[256,1024]{1,0:T(8,128)(2,1)S(1)} %collective-permute-done), channel_id=1, source_target_pairs={{0,1},{1,2},{2,3},{3,0},{4,5},{5,6},{6,7},{7,4},{8,9},{9,10},{10,1... | collective-permute-start | bytes 1572872 | tf_op jit(solution)/shard_map/ppermute | solution.py:19
  166.2 9.4 %collective-permute-start.2 = (bf16[256,1024]{1,0:T(8,128)(2,1)}, bf16[256,1024]{1,0:T(8,128)(2,1)}, u32[]{:S(2)}, u32[]{:S(2)}) collective-permute-start(bf16[256,1024]{1,0:T(8,128)(2,1)} %collective-permute-done.1), channel_id=1, source_target_pairs={{0,1},{1,2},{2,3},{3,0},{4,5},{5,6},{6,7},{7,4},{8,9},{9,10},{10,1... | collective-permute-start | bytes 1572872 | tf_op jit(solution)/shard_map/ppermute | solution.py:19
  270.3 9.0 %copy-start.24 = (bf16[1024,2,656]{0,2,1:T(8,128)(2,1)S(1)}, bf16[1024,2,656]{0,2,1:T(8,128)(2,1)}, u32[]{:S(2)}) copy-start(bf16[1024,2,656]{0,2,1:T(8,128)(2,1)} %all-gather.11.cloned.1.call-done) | copy-start | bytes 8060932
  277.8 1.1 copy-start.26
  277.8 1.5 copy-start.27
  279.3 36.3 %copy-start.2 = (bf16[256,1024]{1,0:T(8,128)(2,1)S(1)}, bf16[256,1024]{1,0:T(8,128)(2,1)}, u32[]{:S(2)}) copy-start(bf16[256,1024]{1,0:T(8,128)(2,1)} %reduce-scatter.17.cloned.1.call-done) | copy-start | bytes 1572868
  279.3 37.9 %copy-start.4 = (bf16[256,1024]{1,0:T(8,128)(2,1)S(1)}, bf16[256,1024]{1,0:T(8,128)(2,1)}, u32[]{:S(2)}) copy-start(bf16[256,1024]{1,0:T(8,128)(2,1)} %param.21) | copy-start | bytes 1572868
  284.0 58.4 %all-gather.17.cloned.1.call-start = ((), (), s32[]{:S(2)}) async-start(), calls=%async_computation.16 | async-start | bytes 2621440 | tf_op jit(solution)/shard_map/all_gather | solution.py:255
  319.6 186.7 %reduce-scatter.31.cloned.1.call-start = ((), (), s32[]{:S(2)}) async-start(), calls=%async_computation.21 | async-start | bytes 1769472
  326.9 181.4 %reduce-scatter.29.cloned.1.call-start = ((), (), s32[]{:S(2)}) async-start(), calls=%async_computation.20 | async-start | bytes 3244032
  338.7 9.0 %copy-start.8 = (bf16[256,1024]{1,0:T(8,128)(2,1)S(1)}, bf16[256,1024]{1,0:T(8,128)(2,1)}, u32[]{:S(2)}) copy-start(bf16[256,1024]{1,0:T(8,128)(2,1)} %copy-done.7) | copy-start | bytes 1572868
  338.8 212.5 %reduce-scatter.27.cloned.1.call-start = ((), (), s32[]{:S(2)}) async-start(), calls=%async_computation.19 | async-start | bytes 589824
  350.8 136.7 %copy-start.13 = (f32[1024,32]{0,1:T(8,128)S(1)}, f32[1024,32]{0,1:T(8,128)}, u32[]{:S(2)}) copy-start(f32[1024,32]{0,1:T(8,128)} %copy-done.12) | copy-start | bytes 393220
  350.8 136.7 %copy-start.15 = (f32[1024,32]{0,1:T(8,128)S(1)}, f32[1024,32]{0,1:T(8,128)}, u32[]{:S(2)}) copy-start(f32[1024,32]{0,1:T(8,128)} %copy-done.14) | copy-start | bytes 393220
  354.6 1.3 copy-start.6
  355.9 3.6 copy-start
  420.9 1.3 copy-start.6
  422.2 5.0 copy-start
  487.4 131.0 %reduce-scatter.25.cloned.1.call-start = ((), (), s32[]{:S(2)}) async-start(), calls=%async_computation.18 | async-start | bytes 1769472
  489.1 1.9 copy-start.25
  490.8 3.1 copy-start.10
  493.9 2.8 copy-start.11
  496.7 154.8 %reduce-scatter.23.cloned.1.call-start = ((), (), s32[]{:S(2)}) async-start(), calls=%async_computation.17 | async-start | bytes 2621440 | tf_op jit(solution)/shard_map/reduce_scatter | solution.py:282
  501.3 191.2 %reduce-scatter.19.cloned.1.call-start = ((), (), s32[]{:S(2)}) async-start(), calls=%async_computation.13 | async-start | bytes 2621440 | tf_op jit(solution)/shard_map/reduce_scatter | solution.py:233
  506.3 145.2 %copy-start.19 = (f32[1024]{0:T(1024)S(1)}, f32[1024]{0:T(1024)}, u32[]{:S(2)}) copy-start(f32[1024]{0:T(1024)} %param.14) | copy-start | bytes 12292
  506.3 145.2 %copy-start.21 = (f32[256]{0:T(256)S(1)}, f32[256]{0:T(256)}, u32[]{:S(2)}) copy-start(f32[256]{0:T(256)} %copy-done.20) | copy-start | bytes 3076
  506.3 145.2 %copy-start.23 = (f32[256]{0:T(256)S(1)}, f32[256]{0:T(256)}, u32[]{:S(2)}) copy-start(f32[256]{0:T(256)} %copy-done.22) | copy-start | bytes 3076
  506.3 186.3 %copy-start.3 = (bf16[256,1024]{1,0:T(8,128)(2,1)S(1)}, bf16[256,1024]{1,0:T(8,128)(2,1)}, u32[]{:S(2)}) copy-start(bf16[256,1024]{1,0:T(8,128)(2,1)} %reduce-scatter.21.cloned.1.call-done) | copy-start | bytes 1572868
  506.3 186.3 %copy-start.5 = (bf16[256,1024]{1,0:T(8,128)(2,1)S(1)}, bf16[256,1024]{1,0:T(8,128)(2,1)}, u32[]{:S(2)}) copy-start(bf16[256,1024]{1,0:T(8,128)(2,1)} %param.21) | copy-start | bytes 1572868
  (1 other events, 0.6 us)
Sparse Core Ops, SparseCore 0:
  10.0 51.3 all-gather.8
  63.6 21.1 all-gather.6
  113.4 31.4 reduce-scatter.16
  147.0 57.6 all-gather.10
  206.7 40.7 all-gather.12
  249.1 21.2 all-gather.14
  284.1 31.4 reduce-scatter.20
  319.8 22.5 all-gather.16
  345.8 64.9 reduce-scatter.30
  414.6 71.0 reduce-scatter.28
  490.0 61.2 reduce-scatter.26
  554.5 63.8 reduce-scatter.24
  621.1 30.3 reduce-scatter.22
  653.9 31.4 reduce-scatter.18
